TPU v7x, 32 devices: a whole 2x2x4 slice. The times are simulated.
32 devices in a mesh: fsdp: 4 (over y, core), tensor: 8 (over z, x).
Axes of the slice: x: 2, y: 2, z: 4, core: 2. Of those that a mesh axis runs over, the one named last changes fastest.
Arguments:
- activations: bfloat16 [4096, 8192], P('fsdp', 'tensor'), may hold values from -6 to 6
- first_factor: bfloat16 [64, 128, 512], P('tensor', 'fsdp'), may hold values from -0.5 to 0.5
- second_factor: bfloat16 [64, 512, 512], P('tensor', 'fsdp'), may hold values from -0.25 to 0.25
- third_factor: bfloat16 [64, 512, 512], P('tensor', 'fsdp'), may hold values from -0.25 to 0.25
- fourth_factor: bfloat16 [64, 512, 128], P('tensor', 'fsdp'), may hold values from -0.25 to 0.25
- out_grad: bfloat16 [4096, 8192], P('fsdp', 'tensor'), may hold values from -6 to 6
Outputs:
- result: bfloat16 [4096, 8192], P('fsdp', 'tensor')
- in_grad: bfloat16 [4096, 8192], P('fsdp', 'tensor')
- first_grad: float32 [64, 128, 512], P('tensor', 'fsdp')
- second_grad: float32 [64, 512, 512], P('tensor', 'fsdp')
- third_grad: float32 [64, 512, 512], P('tensor', 'fsdp')
- fourth_grad: float32 [64, 512, 128], P('tensor', 'fsdp')
All inputs are finite; a program needn't handle non-finite values.
Results may differ from a plain program's by a relative error of at most 0.014.
Values may be sent and summed in bfloat16 or wider, within the bound.
A program may use at most 128 MiB of HBM per device.

v0:
```python
import jax
import jax.numpy as jnp
from jax import lax
from jax.sharding import PartitionSpec as P

D = 8192
NB = 64
HB = 512


def gelu_value(v):
    return 0.5 * v * (1.0 + lax.erf(v * 0.7071067811865476))


def gelu_slope(v):
    return (
        0.5 * (1.0 + lax.erf(v * 0.7071067811865476))
        + v * jnp.exp(-0.5 * v * v) * 0.3989422804014327
    )


def fetch_first(shard):
    return lax.all_gather(shard, "fsdp", axis=1, tiled=True)


def fetch_second(shard):
    return lax.all_gather(shard, "fsdp", axis=1, tiled=True)


def fetch_third(shard):
    return lax.all_gather(shard, "fsdp", axis=1, tiled=True)


def fetch_fourth(shard):
    return lax.all_gather(shard, "fsdp", axis=1, tiled=True)


def split_units(arr):
    return arr.reshape(arr.shape[0], NB, HB // NB, arr.shape[2])


def join_units(received):
    local_blocks = received.shape[1]
    return received.transpose(1, 0, 2, 3).reshape(local_blocks, HB, received.shape[3])


def local(activations, first_factor, second_factor, third_factor, fourth_factor, out_grad):
    f32 = jnp.float32
    bf16 = jnp.bfloat16
    tok = activations.shape[0]
    local_blocks = second_factor.shape[0]
    block_in = D // NB
    inputs = activations.reshape(tok, local_blocks, block_in)
    factors = (
        fetch_first(first_factor),
        fetch_second(second_factor),
        fetch_third(third_factor),
        fetch_fourth(fourth_factor),
    )
    wone, wtwo, wthree, wfour = factors
    first_out = jnp.einsum("tbi,bij->bjt", inputs, wone, preferred_element_type=f32).astype(bf16)
    mixed_part = join_units(
        lax.all_to_all(split_units(first_out), "tensor", split_axis=1, concat_axis=0, tiled=True)
    )
    pre_part = jnp.einsum("cpt,cpm->cmt", mixed_part, wtwo, preferred_element_type=f32)
    hidden_part = gelu_value(pre_part).astype(bf16)
    down_part = jnp.einsum("cmt,cmn->cnt", hidden_part, wthree, preferred_element_type=f32).astype(
        bf16
    )
    back = lax.all_to_all(split_units(down_part), "tensor", split_axis=1, concat_axis=0, tiled=True)
    regrouped = join_units(back)
    result = jnp.einsum("bpt,bpo->tbo", regrouped, wfour, preferred_element_type=f32).astype(bf16)
    result = result.reshape(tok, local_blocks * block_in)
    vone, vtwo, vthree, vfour = (
        fetch_first(first_factor),
        fetch_second(second_factor),
        fetch_third(third_factor),
        fetch_fourth(fourth_factor),
    )
    grad_out = out_grad.reshape(tok, local_blocks, block_in)
    fourth_grad = jnp.einsum("bpt,tbo->bpo", regrouped, grad_out, preferred_element_type=f32)
    dw = jnp.einsum("tbo,bpo->bpt", grad_out, vfour, preferred_element_type=f32).astype(bf16)
    ddown = join_units(
        lax.all_to_all(split_units(dw), "tensor", split_axis=1, concat_axis=0, tiled=True)
    )
    again_out = jnp.einsum("tbi,bij->bjt", inputs, vone, preferred_element_type=f32).astype(bf16)
    mixed_in = join_units(
        lax.all_to_all(split_units(again_out), "tensor", split_axis=1, concat_axis=0, tiled=True)
    )
    pre = jnp.einsum("cpt,cpm->cmt", mixed_in, vtwo, preferred_element_type=f32)
    hidden = gelu_value(pre).astype(bf16)
    third_grad = jnp.einsum("cmt,cnt->cmn", hidden, ddown, preferred_element_type=f32)
    dhidden = jnp.einsum("cnt,cmn->cmt", ddown, vthree, preferred_element_type=f32)
    dpre = (dhidden * gelu_slope(pre)).astype(bf16)
    second_grad = jnp.einsum("cpt,cmt->cpm", mixed_in, dpre, preferred_element_type=f32)
    dz = jnp.einsum("cmt,cpm->cpt", dpre, vtwo, preferred_element_type=f32).astype(bf16)
    dy = join_units(
        lax.all_to_all(split_units(dz), "tensor", split_axis=1, concat_axis=0, tiled=True)
    )
    first_grad = jnp.einsum("tbi,bjt->bij", inputs, dy, preferred_element_type=f32)
    in_grad = jnp.einsum("bjt,bij->tbi", dy, vone, preferred_element_type=f32).astype(bf16)
    in_grad = in_grad.reshape(tok, local_blocks * block_in)
    shares = (
        lax.psum_scatter(
            first_grad.astype(jnp.bfloat16), "fsdp", scatter_dimension=1, tiled=True
        ).astype(jnp.float32),
        lax.psum_scatter(
            second_grad.astype(jnp.bfloat16), "fsdp", scatter_dimension=1, tiled=True
        ).astype(jnp.float32),
        lax.psum_scatter(
            third_grad.astype(jnp.bfloat16), "fsdp", scatter_dimension=1, tiled=True
        ).astype(jnp.float32),
        lax.psum_scatter(
            fourth_grad.astype(jnp.bfloat16), "fsdp", scatter_dimension=1, tiled=True
        ).astype(jnp.float32),
    )
    return (result, in_grad, shares[0], shares[1], shares[2], shares[3])


def solution(mesh):
    in_specs = (
        P("fsdp", "tensor"),
        P("tensor", "fsdp", None),
        P("tensor", "fsdp", None),
        P("tensor", "fsdp", None),
        P("tensor", "fsdp", None),
        P("fsdp", "tensor"),
    )
    out_specs = (
        P("fsdp", "tensor"),
        P("fsdp", "tensor"),
        P("tensor", "fsdp", None),
        P("tensor", "fsdp", None),
        P("tensor", "fsdp", None),
        P("tensor", "fsdp", None),
    )
    return jax.shard_map(local, mesh=mesh, in_specs=in_specs, out_specs=out_specs, check_vma=False)
```

profile of v0, /device:TPU:16, one launch (start us, length us, event | category | flops | bytes accessed | tf_op | source)
XLA Modules:
  0.0 899.8 jit_solution(2316316129718884985)
XLA Ops:
  9.2 18.9 %all-gather.11.cloned.1.call-done = bf16[8,512,128]{1,2,0:T(8,128)(2,1)} async-done(((bf16[8,128,128]{1,2,0:T(8,128)(2,1)}), bf16[8,512,128]{1,2,0:T(8,128)(2,1)}) %all-gather.11.cloned.1.call-update) | async-done | bytes 1048592 | tf_op jit(solution)/shard_map/all_gather | solution.py:35
  28.1 7.6 convert_bitcast_fusion.1
  35.7 8.1 copy.65
  50.5 18.4 %all-gather.5.cloned.1.call-done = bf16[8,128,512]{2,1,0:T(8,128)(2,1)} async-done(((bf16[8,32,512]{2,1,0:T(8,128)(2,1)}), bf16[8,128,512]{2,1,0:T(8,128)(2,1)}) %all-gather.5.cloned.1.call-update) | async-done | bytes 1048592 | tf_op jit(solution)/shard_map/all_gather | solution.py:23
  68.9 6.8 convert_bitcast_fusion.3
  75.8 8.0 copy.55
  83.8 146.2 %all-to-all-done.2 = bf16[8,64,8,1024]{3,2,0,1:T(8,128)(2,1)} async-done(((bf16[8,64,8,1024]{3,2,0,1:T(8,128)(2,1)}), bf16[8,64,8,1024]{3,2,0,1:T(8,128)(2,1)}, u32[]{:S(2)}, u32[]{:S(2)}) %all-to-all-start.2) | async-done | bytes 8388640 | tf_op jit(solution)/shard_map/all_to_all | solution.py:84
  230.0 8.2 all-to-all-start
  240.5 8.8 copy.66
  249.4 168.3 %all-to-all-done = bf16[8,64,8,1024]{3,2,0,1:T(8,128)(2,1)} async-done(((bf16[8,64,8,1024]{3,2,0,1:T(8,128)(2,1)}), bf16[8,64,8,1024]{3,2,0,1:T(8,128)(2,1)}, u32[]{:S(2)}, u32[]{:S(2)}) %all-to-all-start) | async-done | bytes 8388640 | tf_op jit(solution)/shard_map/all_to_all | solution.py:63
  417.6 8.5 copy.56
  426.1 14.5 %fusion.7 = (bf16[8,512,1024]{1,2,0:T(8,128)(2,1)}, f32[8,1024,512]{2,1,0:T(8,128)}) fusion(bf16[8,512,1024]{2,1,0:T(8,128)(2,1)} %bitcast.126, bf16[8,512,512]{2,1,0:T(8,128)(2,1)} %all-gather.7.cloned.1.call-done), kind=kOutput, calls=%fused_computation.10 | convolution fusion | flops 4315938816 | bytes 37748736 | tf_op jit(solution)/shard_map/cpt,cpm->cmt/dot_general | solution.py:65
  440.6 14.3 %fusion.5 = bf16[8,512,1024]{1,2,0:T(8,128)(2,1)S(1)} fusion(f32[8,1024,512]{2,1,0:T(8,128)} %get-tuple-element.25, bf16[8,512,1024]{2,1,0:T(8,128)(2,1)} %bitcast.128, bf16[8,512,512]{1,2,0:T(8,128)(2,1)} %all-gather.9.cloned.1.call-done), kind=kOutput, calls=%fused_computation.6 | convolution fusion | flops 4336910336 | bytes 37748736 | tf_op jit(solution)/shard_map/cnt,cmn->cmt/dot_general | solution.py:93
  464.8 8.0 copy.70
  472.9 8.3 all-to-all-start.3
  481.4 11.0 %convolution_convert_fusion = bf16[8,512,512]{2,1,0:T(8,128)(2,1)} fusion(bf16[8,512,1024]{1,2,0:T(8,128)(2,1)} %get-tuple-element.24, bf16[8,512,1024]{2,1,0:T(8,128)(2,1)} %bitcast.129), kind=kOutput, calls=%fused_computation.17 | convolution fusion | flops 4297064448 | bytes 20971520 | tf_op jit(solution)/shard_map/cmt,cnt->cmn/dot_general | solution.py:92
  492.4 10.3 %convert_bitcast_fusion.2 = bf16[8,64,8,1024]{3,2,1,0:T(8,128)(2,1)} fusion(bf16[8,512,1024]{1,2,0:T(8,128)(2,1)} %get-tuple-element.24, bf16[8,512,512]{1,2,0:T(8,128)(2,1)} %all-gather.9.cloned.1.call-done), kind=kOutput, calls=%fused_computation.15 | convolution fusion | flops 4299161600 | bytes 20971520 | tf_op jit(solution)/shard_map/cmt,cmn->cnt/dot_general | solution.py:67
  502.8 8.3 copy.60
  511.1 148.8 %all-to-all-done.3 = bf16[8,64,8,1024]{3,2,0,1:T(8,128)(2,1)} async-done(((bf16[8,64,8,1024]{3,2,0,1:T(8,128)(2,1)}), bf16[8,64,8,1024]{3,2,0,1:T(8,128)(2,1)}, u32[]{:S(2)}, u32[]{:S(2)}) %all-to-all-start.3) | async-done | bytes 8388640 | tf_op jit(solution)/shard_map/all_to_all | solution.py:98
  659.8 8.2 all-to-all-start.1
  668.1 12.2 %convolution_convert_fusion.1 = bf16[8,512,512]{2,1,0:T(8,128)(2,1)} fusion(bf16[8,512,1024]{2,1,0:T(8,128)(2,1)} %bitcast.127, bf16[8,512,1024]{1,2,0:T(8,128)(2,1)} %copy-done.5), kind=kOutput, calls=%fused_computation.18 | convolution fusion | flops 4297064448 | bytes 20971520 | tf_op jit(solution)/shard_map/cpt,cmt->cpm/dot_general | solution.py:95
  680.6 9.2 %copy.71 = bf16[8,8,8,8,1024]{4,3,1,0,2:T(8,128)(2,1)} copy(bf16[8,8,8,8,1024]{4,3,1,2,0:T(8,128)(2,1)} %bitcast.26) | data formatting | bytes 16777216 | tf_op jit(solution)/shard_map/all_to_all | solution.py:98
  697.7 149.3 %all-to-all-done.1 = bf16[8,64,8,1024]{3,2,0,1:T(8,128)(2,1)} async-done(((bf16[8,64,8,1024]{3,2,0,1:T(8,128)(2,1)}), bf16[8,64,8,1024]{3,2,0,1:T(8,128)(2,1)}, u32[]{:S(2)}, u32[]{:S(2)}) %all-to-all-start.1) | async-done | bytes 8388640 | tf_op jit(solution)/shard_map/all_to_all | solution.py:70
  847.0 8.5 copy.61
  (49 shorter events, 66.3 us)
Async XLA Ops:
  7.2 61.7 %copy-start = (bf16[1024,1024]{1,0:T(8,128)(2,1)S(1)}, bf16[1024,1024]{1,0:T(8,128)(2,1)}, u32[]{:S(2)}) copy-start(bf16[1024,1024]{1,0:T(8,128)(2,1)} %param.6) | copy-start | bytes 6291460
  7.2 20.9 %all-gather.11.cloned.1.call-start = ((), (), s32[]{:S(2)}) async-start(), calls=%async_computation.11 | async-start | bytes 1310720 | tf_op jit(solution)/shard_map/all_gather | solution.py:35
  43.8 186.2 %all-to-all-start.2 = ((bf16[8,64,8,1024]{3,2,0,1:T(8,128)(2,1)}), bf16[8,64,8,1024]{3,2,0,1:T(8,128)(2,1)}, u32[]{:S(2)}, u32[]{:S(2)}) async-start(bf16[8,64,8,1024]{3,2,0,1:T(8,128)(2,1)} %copy.65), calls=%async_computation.2 | async-start | bytes 16777216 | tf_op jit(solution)/shard_map/all_to_all | solution.py:84
  49.8 19.1 %all-gather.5.cloned.1.call-start = ((), (), s32[]{:S(2)}) async-start(), calls=%async_computation.8 | async-start | bytes 1310720 | tf_op jit(solution)/shard_map/all_gather | solution.py:23
  83.8 155.4 %copy-start.3 = (bf16[8,128,512]{2,1,0:T(8,128)(2,1)S(1)}, bf16[8,128,512]{2,1,0:T(8,128)(2,1)}, u32[]{:S(2)}) copy-start(bf16[8,128,512]{2,1,0:T(8,128)(2,1)} %param.9) | copy-start | bytes 3145732
  230.0 187.6 %all-to-all-start = ((bf16[8,64,8,1024]{3,2,0,1:T(8,128)(2,1)}), bf16[8,64,8,1024]{3,2,0,1:T(8,128)(2,1)}, u32[]{:S(2)}, u32[]{:S(2)}) async-start(bf16[8,64,8,1024]{3,2,0,1:T(8,128)(2,1)} %copy.55), calls=%async_computation | async-start | bytes 16777216 | tf_op jit(solution)/shard_map/all_to_all | solution.py:63
  238.2 187.8 %all-gather.7.cloned.1.call-start = ((), (), s32[]{:S(2)}) async-start(), calls=%async_computation.9 | async-start | bytes 5242880 | tf_op jit(solution)/shard_map/all_gather | solution.py:27
  239.0 201.6 %all-gather.9.cloned.1.call-start = ((), (), s32[]{:S(2)}) async-start(), calls=%async_computation.10 | async-start | bytes 5242880 | tf_op jit(solution)/shard_map/all_gather | solution.py:31
  440.6 17.5 %copy-start.4 = (bf16[8,512,512]{2,1,0:T(8,128)(2,1)S(1)}, bf16[8,512,512]{2,1,0:T(8,128)(2,1)}, u32[]{:S(2)}) copy-start(bf16[8,512,512]{2,1,0:T(8,128)(2,1)} %all-gather.7.cloned.1.call-done) | copy-start | bytes 12582916
  454.8 3.3 copy-start.5
  472.9 187.0 %all-to-all-start.3 = ((bf16[8,64,8,1024]{3,2,0,1:T(8,128)(2,1)}), bf16[8,64,8,1024]{3,2,0,1:T(8,128)(2,1)}, u32[]{:S(2)}, u32[]{:S(2)}) async-start(bf16[8,64,8,1024]{3,2,0,1:T(8,128)(2,1)} %copy.70), calls=%async_computation.3 | async-start | bytes 16777216 | tf_op jit(solution)/shard_map/all_to_all | solution.py:98
  481.2 381.2 %reduce-scatter.9.cloned.1.call-start = ((), (), s32[]{:S(2)}) async-start(), calls=%async_computation.14 | async-start | bytes 5242880 | tf_op jit(solution)/shard_map/reduce_scatter | solution.py:110
  659.8 187.2 %all-to-all-start.1 = ((bf16[8,64,8,1024]{3,2,0,1:T(8,128)(2,1)}), bf16[8,64,8,1024]{3,2,0,1:T(8,128)(2,1)}, u32[]{:S(2)}, u32[]{:S(2)}) async-start(bf16[8,64,8,1024]{3,2,0,1:T(8,128)(2,1)} %copy.60), calls=%async_computation.1 | async-start | bytes 16777216 | tf_op jit(solution)/shard_map/all_to_all | solution.py:70
  668.1 197.1 %reduce-scatter.7.cloned.1.call-start = ((), (), s32[]{:S(2)}) async-start(), calls=%async_computation.13 | async-start | bytes 5242880 | tf_op jit(solution)/shard_map/reduce_scatter | solution.py:107
  680.3 208.6 %reduce-scatter.5.cloned.1.call-start = ((), (), s32[]{:S(2)}) async-start(), calls=%async_computation.12 | async-start | bytes 1310720 | tf_op jit(solution)/shard_map/reduce_scatter | solution.py:104
  697.6 193.1 %reduce-scatter.11.cloned.1.call-start = ((), (), s32[]{:S(2)}) async-start(), calls=%async_computation.15 | async-start | bytes 1310720 | tf_op jit(solution)/shard_map/reduce_scatter | solution.py:113
  847.0 8.6 copy-start.2
  868.0 10.8 %copy-start.1 = (bf16[8,512,128]{1,2,0:T(8,128)(2,1)S(1)}, bf16[8,512,128]{1,2,0:T(8,128)(2,1)}, u32[]{:S(2)}) copy-start(bf16[8,512,128]{1,2,0:T(8,128)(2,1)} %all-gather.11.cloned.1.call-done) | copy-start | bytes 3145732
Sparse Core Ops, SparseCore 0:
  10.1 17.9 all-gather.10
  52.2 16.6 all-gather.4
  240.6 34.4 all-gather.6
  277.1 35.0 all-gather.8
  492.6 44.4 reduce-scatter.8
  680.4 44.4 reduce-scatter.6
  727.5 24.8 reduce-scatter.4
  862.5 26.0 reduce-scatter.10
where the time goes:
time: 911 us; the launch traced here: 900 us
  waiting for transfers between devices  651 us (71%)
  matrix products  109 us (12%)
  local copies, waits for them, and re-layouts  85.5 us (9%)
  starting transfers between devices  31.6 us (3%)
  between operations  14.6 us (2%)
    all_to_all x1, waiting for transfers between devices, local(): lax.all_to_all(split_units(first_out), 'tensor', split_axis=1, concat_axi...  168 us
    all_to_all x1, waiting for transfers between devices, local(): lax.all_to_all(split_units(down_part), 'tensor', split_axis=1, concat_axi...  149 us
    all_to_all x1, waiting for transfers between devices, local(): lax.all_to_all(split_units(dz), 'tensor', split_axis=1, concat_axis=0, ti...  149 us
    all_to_all x1, waiting for transfers between devices, local(): lax.all_to_all(split_units(dw), 'tensor', split_axis=1, concat_axis=0, ti...  146 us
    reshape x4, local copies, waits for them, and re-layouts, split_units(): return arr.reshape(arr.shape[0], NB, HB // NB, arr.shape[2])  32.5 us
    all_gather x1, waiting for transfers between devices, fetch_fourth(): return lax.all_gather(shard, 'fsdp', axis=1, tiled=True)  18.9 us
    all_gather x1, waiting for transfers between devices, fetch_first(): return lax.all_gather(shard, 'fsdp', axis=1, tiled=True)  18.4 us
  transfers between devices with their start and end apart: 12, of which 6 were waited for; matrix products, arithmetic and copies ran while one was open for 17% of the time, Pallas kernels for 0%

commit v1 on v0

v1 whole, which is shorter than its diff:
```python
import jax
import jax.numpy as jnp
from jax import lax
from jax.sharding import PartitionSpec as P

D = 8192
NB = 64
HB = 512
F32 = jnp.float32
BF16 = jnp.bfloat16


def gelu_both(v):
    half = 0.5 * (1.0 + lax.erf(v * 0.7071067811865476))
    slope = half + v * jnp.exp(-0.5 * v * v) * 0.3989422804014327
    return v * half, slope


def fetch(shard):
    return lax.all_gather(shard, "fsdp", axis=1, tiled=True)


def split_units(arr):
    blocks, units, tok = arr.shape
    return arr.reshape(blocks, NB, units // NB, tok).transpose(1, 0, 2, 3)


def send(parts):
    return lax.all_to_all(parts, "tensor", split_axis=0, concat_axis=0, tiled=True)


def join_halves(halves, groups):
    parts = [h.reshape(groups, -1, *h.shape[1:]) for h in halves]
    arr = parts[0] if len(parts) == 1 else jnp.concatenate(parts, axis=2)
    own, tok = arr.shape[1], arr.shape[4]
    return arr.transpose(1, 0, 2, 3, 4).reshape(own, HB, tok)


def follow(value, done):
    return lax.optimization_barrier((value, done))


def scatter(grad):
    return lax.psum_scatter(
        grad.astype(BF16), "fsdp", scatter_dimension=1, tiled=True
    ).astype(F32)


def local(activations, first_factor, second_factor, third_factor, fourth_factor, out_grad):
    tok = activations.shape[0]
    local_blocks = second_factor.shape[0]
    block_in = D // NB
    inputs = activations.reshape(tok, local_blocks, block_in)
    grad_out = out_grad.reshape(tok, local_blocks, block_in)
    groups = NB // local_blocks
    pieces = 2 if local_blocks % 2 == 0 else 1
    part = local_blocks // pieces
    spans = [slice(n * part, (n + 1) * part) for n in range(pieces)]
    wones = [fetch(first_factor[s]) for s in spans]
    wfour = fetch(fourth_factor)
    wtwo = fetch(second_factor)
    wthree = fetch(third_factor)
    received = []
    for s, w in zip(spans, wones):
        out = jnp.einsum("tbi,bij->bjt", inputs[:, s], w, preferred_element_type=F32).astype(BF16)
        received.append(send(split_units(out)))
    dw = jnp.einsum("tbo,bpo->bpt", grad_out, wfour, preferred_element_type=F32).astype(BF16)
    dw, received[-1] = follow(split_units(dw), received[-1])
    ddown_raw = send(dw)
    mixed = join_halves(received, groups)
    pre = jnp.einsum("cpt,cpm->cmt", mixed, wtwo, preferred_element_type=F32)
    act, slope = gelu_both(pre)
    hidden = act.astype(BF16)
    down = jnp.einsum("cmt,cmn->cnt", hidden, wthree, preferred_element_type=F32).astype(BF16)
    down, ddown_raw = follow(split_units(down), ddown_raw)
    regrouped_raw = send(down)
    ddown = join_halves([ddown_raw], groups)
    dhidden = jnp.einsum("cnt,cmn->cmt", ddown, wthree, preferred_element_type=F32)
    dpre = (dhidden * slope).astype(BF16)
    dz = jnp.einsum("cmt,cpm->cpt", dpre, wtwo, preferred_element_type=F32).astype(BF16)
    third_grad = jnp.einsum("cmt,cnt->cmn", hidden, ddown, preferred_element_type=F32)
    second_grad = jnp.einsum("cpt,cmt->cpm", mixed, dpre, preferred_element_type=F32)
    by_half = dz.reshape(local_blocks, groups, pieces, part * (HB // NB), tok)
    outs = [
        by_half[:, :, n]
        .reshape(local_blocks, groups * part, HB // NB, tok)
        .transpose(1, 0, 2, 3)
        for n in range(pieces)
    ]
    (outs, regrouped_raw) = follow(outs, regrouped_raw)
    in_parts, first_parts = [], []
    for n, (s, w) in enumerate(zip(spans, wones)):
        dy = join_halves([send(outs[n])], groups)
        grad = jnp.einsum("tbi,bjt->bij", inputs[:, s], dy, preferred_element_type=F32)
        first_parts.append(grad.astype(BF16))
        in_parts.append(
            jnp.einsum("bjt,bij->tbi", dy, w, preferred_element_type=F32)
            .astype(BF16)
            .reshape(tok, part * block_in)
        )
    regrouped = join_halves([regrouped_raw], groups)
    result = jnp.einsum("bpt,bpo->tbo", regrouped, wfour, preferred_element_type=F32).astype(BF16)
    result = result.reshape(tok, local_blocks * block_in)
    fourth_grad = jnp.einsum("bpt,tbo->bpo", regrouped, grad_out, preferred_element_type=F32)
    return (
        result,
        jnp.concatenate(in_parts, axis=1),
        scatter(jnp.concatenate(first_parts, axis=0)),
        scatter(second_grad),
        scatter(third_grad),
        scatter(fourth_grad),
    )


def solution(mesh):
    in_specs = (
        P("fsdp", "tensor"),
        P("tensor", "fsdp", None),
        P("tensor", "fsdp", None),
        P("tensor", "fsdp", None),
        P("tensor", "fsdp", None),
        P("fsdp", "tensor"),
    )
    out_specs = (
        P("fsdp", "tensor"),
        P("fsdp", "tensor"),
        P("tensor", "fsdp", None),
        P("tensor", "fsdp", None),
        P("tensor", "fsdp", None),
        P("tensor", "fsdp", None),
    )
    return jax.shard_map(local, mesh=mesh, in_specs=in_specs, out_specs=out_specs, check_vma=False)
```

time: 911 us -> 852 us (0.935)
  waiting for transfers between devices: 651 us -> 545 us
  starting transfers between devices: 31.6 us -> 47.4 us
  blocking collectives: 0 us -> 14 us
  other arithmetic: 7.43 us -> 18.2 us
    all_to_all x4 -> x6, waiting for transfers between devices: 613 us -> 484 us  [send(): lax.all_to_all(parts, 'tensor', split_axis=0, concat_axis=0, tiled=True)]
    all_to_all x4 -> x0, local copies, waits for them, and re-layouts: 35 us -> none  [the longest x1 9.19 us: local(): lax.all_to_all(split_units(dz), 'tensor', split_axis=1, concat_axis=0, ti...]
    transpose x0 -> x5, local copies, waits for them, and re-layouts: none -> 33.8 us  [join_halves(): return arr.transpose(1, 0, 2, 3, 4).reshape(own, HB, tok)]
    all_gather x4 -> x3, waiting for transfers between devices: 37.3 us -> 59.3 us  [fetch(): return lax.all_gather(shard, 'fsdp', axis=1, tiled=True)]
    all_to_all x4 -> x6, starting transfers between devices: 30.8 us -> 46.1 us  [send(): lax.all_to_all(parts, 'tensor', split_axis=0, concat_axis=0, tiled=True)]
    all_gather x0 -> x2, blocking collectives: none -> 14 us  [fetch(): return lax.all_gather(shard, 'fsdp', axis=1, tiled=True)]
    optimization_barrier x0 -> x2, local copies, waits for them, and re-layouts: none -> 9.62 us  [follow(): return lax.optimization_barrier((value, done))]
    reshape x4 -> x6, local copies, waits for them, and re-layouts: 32.5 us -> 23.7 us  [the longest x4 21 us: split_units(): return arr.reshape(blocks, NB, units // NB, tok).transpose(1, 0, 2, 3)]
  transfers between devices with their start and end apart: 12 -> 13, of which waited for: 6 -> 9; matrix products, arithmetic and copies ran while one was open for 17% -> 24% of each run, Pallas kernels for 0% -> 0%
where the time goes in v1:
time: 852 us; the launch traced here: 840 us
  waiting for transfers between devices  545 us (64%)
  matrix products  113 us (13%)
  local copies, waits for them, and re-layouts  87.8 us (10%)
  starting transfers between devices  47.4 us (6%)
  other arithmetic  18.2 us (2%)
  between operations  14.5 us (2%)
  blocking collectives  14 us (2%)
    all_to_all x6, waiting for transfers between devices, send(): lax.all_to_all(parts, 'tensor', split_axis=0, concat_axis=0, tiled=True)  484 us
    all_gather x3, waiting for transfers between devices, fetch(): return lax.all_gather(shard, 'fsdp', axis=1, tiled=True)  59.3 us
    all_to_all x6, starting transfers between devices, send(): lax.all_to_all(parts, 'tensor', split_axis=0, concat_axis=0, tiled=True)  46.1 us
    transpose x5, local copies, waits for them, and re-layouts, join_halves(): return arr.transpose(1, 0, 2, 3, 4).reshape(own, HB, tok)  33.8 us
    reshape x4, local copies, waits for them, and re-layouts, split_units(): return arr.reshape(blocks, NB, units // NB, tok).transpose(1, 0, 2, 3)  21 us
    dot_general x1, matrix products, local(): jnp.einsum('cnt,cmn->cmt', ddown, wthree, preferred_element_type=F32)  18 us
  transfers between devices with their start and end apart: 13, of which 9 were waited for; matrix products, arithmetic and copies ran while one was open for 24% of the time, Pallas kernels for 0%

profile of v1, /device:TPU:16, one launch (start us, length us, event | category | flops | bytes accessed | tf_op | source)
XLA Modules:
  0.0 839.9 jit_solution(9954805708362142884)
XLA Ops:
  43.2 77.9 %all-to-all-done.1 = bf16[64,4,8,1024]{3,2,1,0:T(8,128)(2,1)} async-done(((bf16[64,4,8,1024]{3,2,1,0:T(8,128)(2,1)}), bf16[64,4,8,1024]{3,2,1,0:T(8,128)(2,1)}, u32[]{:S(2)}, u32[]{:S(2)}) %all-to-all-start.1) | async-done | bytes 4194336 | tf_op jit(solution)/shard_map/all_to_all | solution.py:29
  121.1 7.9 all-to-all-start
  129.7 18.9 %all-gather.4.cloned.1.call-done = bf16[8,512,128]{2,1,0:T(8,128)(2,1)} async-done(((bf16[8,128,128]{2,1,0:T(8,128)(2,1)}), bf16[8,512,128]{2,1,0:T(8,128)(2,1)}) %all-gather.4.cloned.1.call-update) | async-done | bytes 1048592 | tf_op jit(solution)/shard_map/all_gather | solution.py:20
  155.5 8.1 copy.142
  163.6 54.9 %all-to-all-done = bf16[64,4,8,1024]{3,2,1,0:T(8,128)(2,1)} async-done(((bf16[64,4,8,1024]{3,2,1,0:T(8,128)(2,1)}), bf16[64,4,8,1024]{3,2,1,0:T(8,128)(2,1)}, u32[]{:S(2)}, u32[]{:S(2)}) %all-to-all-start) | async-done | bytes 4194336 | tf_op jit(solution)/shard_map/all_to_all | solution.py:29
  218.6 8.2 all-to-all-start.2
  236.9 9.3 %copy.89 = bf16[8,8,8,8,1024]{4,3,2,1,0:T(8,128)(2,1)} copy(bf16[8,8,8,8,1024]{4,3,2,0,1:T(8,128)(2,1)} %maximum_bitcast_fusion) | data formatting | bytes 16777216 | tf_op jit(solution)/shard_map/transpose | solution.py:36
  246.3 18.0 %all-gather.6.cloned.1.call-done = bf16[8,512,512]{2,1,0:T(8,128)(2,1)} async-done(((bf16[8,128,512]{2,1,0:T(8,128)(2,1)}), bf16[8,512,512]{2,1,0:T(8,128)(2,1)}) %all-gather.6.cloned.1.call-update) | async-done | bytes 4194320 | tf_op jit(solution)/shard_map/all_gather | solution.py:20
  264.2 14.8 %fusion.9 = (bf16[8,512,1024]{1,2,0:T(8,128)(2,1)}, f32[8,1024,512]{2,1,0:T(8,128)}) fusion(bf16[8,512,1024]{2,1,0:T(8,128)(2,1)} %bitcast.138, bf16[8,512,512]{2,1,0:T(8,128)(2,1)} %all-gather.6.cloned.1.call-done), kind=kOutput, calls=%fused_computation.12 | convolution fusion | flops 4315938816 | bytes 37748736 | tf_op jit(solution)/shard_map/cpt,cpm->cmt/dot_general | solution.py:71
  279.1 22.4 %all-gather.8.cloned.1.call-done = bf16[8,512,512]{1,2,0:T(8,128)(2,1)} async-done(((bf16[8,128,512]{1,2,0:T(8,128)(2,1)}), bf16[8,512,512]{1,2,0:T(8,128)(2,1)}) %all-gather.8.cloned.1.call-update) | async-done | bytes 4194320 | tf_op jit(solution)/shard_map/all_gather | solution.py:20
  301.4 10.2 %convert_bitcast_fusion = bf16[8,64,8,1024]{3,2,1,0:T(8,128)(2,1)} fusion(bf16[8,512,1024]{1,2,0:T(8,128)(2,1)} %get-tuple-element.48, bf16[8,512,512]{1,2,0:T(8,128)(2,1)} %all-gather.8.cloned.1.call-done), kind=kOutput, calls=%fused_computation.16 | convolution fusion | flops 4299161600 | bytes 20971520 | tf_op jit(solution)/shard_map/cmt,cmn->cnt/dot_general | solution.py:74
  311.7 8.1 copy.141
  319.7 85.8 %all-to-all-done.2 = bf16[64,8,8,1024]{3,2,1,0:T(8,128)(2,1)} async-done(((bf16[64,8,8,1024]{3,2,1,0:T(8,128)(2,1)}), bf16[64,8,8,1024]{3,2,1,0:T(8,128)(2,1)}, u32[]{:S(2)}, u32[]{:S(2)}) %all-to-all-start.2) | async-done | bytes 8388640 | tf_op jit(solution)/shard_map/all_to_all | solution.py:29
  405.5 8.2 all-to-all-start.3
  413.9 8.4 %copy.94 = bf16[8,8,8,8,1024]{4,3,2,1,0:T(8,128)(2,1)} copy(bf16[8,8,8,8,1024]{4,3,2,0,1:T(8,128)(2,1)} %bitcast.16) | data formatting | bytes 16777216 | tf_op jit(solution)/shard_map/transpose | solution.py:36
  422.3 11.1 %convolution_convert_fusion.1 = bf16[8,512,512]{2,1,0:T(8,128)(2,1)} fusion(bf16[8,512,1024]{1,2,0:T(8,128)(2,1)} %get-tuple-element.48, bf16[8,512,1024]{2,1,0:T(8,128)(2,1)} %bitcast.140), kind=kOutput, calls=%fused_computation.23 | convolution fusion | flops 4297064448 | bytes 20971520 | tf_op jit(solution)/shard_map/cmt,cnt->cmn/dot_general | solution.py:81
  433.4 18.0 %fusion.5 = bf16[8,512,1024]{1,2,0:T(8,128)(2,1)} fusion(f32[8,1024,512]{2,1,0:T(8,128)} %get-tuple-element.49, bf16[8,512,1024]{2,1,0:T(8,128)(2,1)} %bitcast.141, bf16[8,512,512]{1,2,0:T(8,128)(2,1)} %all-gather.8.cloned.1.call-done), kind=kOutput, calls=%fused_computation.6 | convolution fusion | flops 4336910336 | bytes 37748736 | tf_op jit(solution)/shard_map/cnt,cmn->cmt/dot_general | solution.py:78
  451.4 12.9 %convolution_convert_fusion = bf16[8,1024,512]{1,2,0:T(8,128)(2,1)S(1)} fusion(bf16[8,512,1024]{1,2,0:T(8,128)(2,1)} %fusion.5, bf16[8,512,512]{2,1,0:T(8,128)(2,1)S(1)} %copy-done.8), kind=kOutput, calls=%fused_computation.18 | convolution fusion | flops 4299161600 | bytes 20971520 | tf_op jit(solution)/shard_map/cmt,cpm->cpt/dot_general | solution.py:80
  468.1 124.6 %all-to-all-done.3 = bf16[64,8,8,1024]{3,2,1,0:T(8,128)(2,1)} async-done(((bf16[64,8,8,1024]{3,2,1,0:T(8,128)(2,1)}), bf16[64,8,8,1024]{3,2,1,0:T(8,128)(2,1)}, u32[]{:S(2)}, u32[]{:S(2)}) %all-to-all-start.3) | async-done | bytes 8388640 | tf_op jit(solution)/shard_map/all_to_all | solution.py:29
  605.5 12.3 %convolution_convert_fusion.2 = bf16[8,512,512]{2,1,0:T(8,128)(2,1)} fusion(bf16[8,512,1024]{2,1,0:T(8,128)(2,1)} %bitcast.139, bf16[8,512,1024]{1,2,0:T(8,128)(2,1)} %fusion.5), kind=kOutput, calls=%fused_computation.24 | convolution fusion | flops 4297064448 | bytes 20971520 | tf_op jit(solution)/shard_map/cpt,cmt->cpm/dot_general | solution.py:82
  622.6 72.1 %all-to-all-done.4 = bf16[32,8,8,1024]{3,2,1,0:T(8,128)(2,1)} async-done(((bf16[32,8,8,1024]{3,2,1,0:T(8,128)(2,1)}), bf16[32,8,8,1024]{3,2,1,0:T(8,128)(2,1)}, u32[]{:S(2)}, u32[]{:S(2)}) %all-to-all-start.4) | async-done | bytes 4194336 | tf_op jit(solution)/shard_map/all_to_all | solution.py:29
  694.7 7.9 all-to-all-start.5
  702.6 8.5 %copy.100 = bf16[8,8,8,8,1024]{4,3,2,1,0:T(8,128)(2,1)} copy(bf16[8,8,8,8,1024]{4,3,2,0,1:T(8,128)(2,1)} %bitcast.27) | data formatting | bytes 16777216 | tf_op jit(solution)/shard_map/transpose | solution.py:36
  722.9 68.9 %all-to-all-done.5 = bf16[32,8,8,1024]{3,2,1,0:T(8,128)(2,1)} async-done(((bf16[32,8,8,1024]{3,2,1,0:T(8,128)(2,1)}), bf16[32,8,8,1024]{3,2,1,0:T(8,128)(2,1)}, u32[]{:S(2)}, u32[]{:S(2)}) %all-to-all-start.5) | async-done | bytes 4194336 | tf_op jit(solution)/shard_map/all_to_all | solution.py:29
  (70 shorter events, 128.0 us)
Async XLA Ops:
  7.2 141.5 %copy-start = (bf16[1024,1024]{1,0:T(8,128)(2,1)S(1)}, bf16[1024,1024]{1,0:T(8,128)(2,1)}, u32[]{:S(2)}) copy-start(bf16[1024,1024]{1,0:T(8,128)(2,1)} %param.11) | copy-start | bytes 6291460
  15.5 6.6 copy-start.4
  24.6 96.6 %all-to-all-start.1 = ((bf16[64,4,8,1024]{3,2,1,0:T(8,128)(2,1)}), bf16[64,4,8,1024]{3,2,1,0:T(8,128)(2,1)}, u32[]{:S(2)}, u32[]{:S(2)}) async-start(bf16[64,4,8,1024]{3,2,1,0:T(8,128)(2,1)} %bitcast.135), calls=%async_computation.1 | async-start | bytes 8388608 | tf_op jit(solution)/shard_map/all_to_all | solution.py:29
  37.5 0.8 copy-start.5
  121.1 97.4 %all-to-all-start = ((bf16[64,4,8,1024]{3,2,1,0:T(8,128)(2,1)}), bf16[64,4,8,1024]{3,2,1,0:T(8,128)(2,1)}, u32[]{:S(2)}, u32[]{:S(2)}) async-start(bf16[64,4,8,1024]{3,2,1,0:T(8,128)(2,1)} %bitcast.134), calls=%async_computation | async-start | bytes 8388608 | tf_op jit(solution)/shard_map/all_to_all | solution.py:29
  129.0 19.7 %all-gather.4.cloned.1.call-start = ((), (), s32[]{:S(2)}) async-start(), calls=%async_computation.10 | async-start | bytes 1310720 | tf_op jit(solution)/shard_map/all_gather | solution.py:20
  163.6 64.5 %copy-start.7 = (bf16[8,128,512]{2,1,0:T(8,128)(2,1)S(1)}, bf16[8,128,512]{2,1,0:T(8,128)(2,1)}, u32[]{:S(2)}) copy-start(bf16[8,128,512]{2,1,0:T(8,128)(2,1)} %param.9) | copy-start | bytes 3145732
  218.6 187.0 %all-to-all-start.2 = ((bf16[64,8,8,1024]{3,2,1,0:T(8,128)(2,1)}), bf16[64,8,8,1024]{3,2,1,0:T(8,128)(2,1)}, u32[]{:S(2)}, u32[]{:S(2)}) async-start(bf16[64,8,8,1024]{3,2,1,0:T(8,128)(2,1)} %bitcast.128), calls=%async_computation.2 | async-start | bytes 16777216 | tf_op jit(solution)/shard_map/all_to_all | solution.py:29
  226.8 37.4 %all-gather.6.cloned.1.call-start = ((), (), s32[]{:S(2)}) async-start(), calls=%async_computation.11 | async-start | bytes 5242880 | tf_op jit(solution)/shard_map/all_gather | solution.py:20
  227.5 73.9 %all-gather.8.cloned.1.call-start = ((), (), s32[]{:S(2)}) async-start(), calls=%async_computation.12 | async-start | bytes 5242880 | tf_op jit(solution)/shard_map/all_gather | solution.py:20
  405.5 187.1 %all-to-all-start.3 = ((bf16[64,8,8,1024]{3,2,1,0:T(8,128)(2,1)}), bf16[64,8,8,1024]{3,2,1,0:T(8,128)(2,1)}, u32[]{:S(2)}, u32[]{:S(2)}) async-start(bf16[64,8,8,1024]{3,2,1,0:T(8,128)(2,1)} %bitcast.129), calls=%async_computation.3 | async-start | bytes 16777216 | tf_op jit(solution)/shard_map/all_to_all | solution.py:29
  413.8 387.4 %reduce-scatter.9.cloned.1.call-start = ((), (), s32[]{:S(2)}) async-start(), calls=%async_computation.15 | async-start | bytes 5242880 | tf_op jit(solution)/shard_map/reduce_scatter | solution.py:44
  433.4 18.0 %copy-start.8 = (bf16[8,512,512]{2,1,0:T(8,128)(2,1)S(1)}, bf16[8,512,512]{2,1,0:T(8,128)(2,1)}, u32[]{:S(2)}) copy-start(bf16[8,512,512]{2,1,0:T(8,128)(2,1)} %all-gather.6.cloned.1.call-done) | copy-start | bytes 12582916
  597.4 97.3 %all-to-all-start.4 = ((bf16[32,8,8,1024]{3,2,1,0:T(8,128)(2,1)}), bf16[32,8,8,1024]{3,2,1,0:T(8,128)(2,1)}, u32[]{:S(2)}, u32[]{:S(2)}) async-start(bf16[32,8,8,1024]{3,2,1,0:T(8,128)(2,1)} %copy.102), calls=%async_computation.4 | async-start | bytes 8388608 | tf_op jit(solution)/shard_map/all_to_all | solution.py:29
  605.3 198.8 %reduce-scatter.7.cloned.1.call-start = ((), (), s32[]{:S(2)}) async-start(), calls=%async_computation.14 | async-start | bytes 5242880 | tf_op jit(solution)/shard_map/reduce_scatter | solution.py:44
  694.7 97.1 %all-to-all-start.5 = ((bf16[32,8,8,1024]{3,2,1,0:T(8,128)(2,1)}), bf16[32,8,8,1024]{3,2,1,0:T(8,128)(2,1)}, u32[]{:S(2)}, u32[]{:S(2)}) async-start(bf16[32,8,8,1024]{3,2,1,0:T(8,128)(2,1)} %copy.104), calls=%async_computation.5 | async-start | bytes 8388608 | tf_op jit(solution)/shard_map/all_to_all | solution.py:29
  702.6 114.5 %reduce-scatter.11.cloned.1.call-start = ((), (), s32[]{:S(2)}) async-start(), calls=%async_computation.16 | async-start | bytes 1310720 | tf_op jit(solution)/shard_map/reduce_scatter | solution.py:44
  717.8 113.1 %reduce-scatter.5.cloned.1.call-start = ((), (), s32[]{:S(2)}) async-start(), calls=%async_computation.13 | async-start | bytes 1310720 | tf_op jit(solution)/shard_map/reduce_scatter | solution.py:44
  791.8 3.4 copy-start.1
  791.8 4.9 copy-start.3
  794.7 4.6 copy-start.2
  801.1 5.8 copy-start.6
Sparse Core Ops, SparseCore 0:
  131.4 17.2 all-gather.3
  229.2 35.0 all-gather.5
  266.4 35.0 all-gather.7
  433.5 45.0 reduce-scatter.8
  617.9 45.0 reduce-scatter.6
  717.9 25.4 reduce-scatter.10
  801.2 26.3 reduce-scatter.4

commit v2 on v1

v2 whole, which is shorter than its diff:
```python
import jax
import jax.numpy as jnp
from jax import lax
from jax.sharding import PartitionSpec as P

D = 8192
NB = 64
HB = 512
F32 = jnp.float32
BF16 = jnp.bfloat16


def gelu_both(v):
    half = 0.5 * (1.0 + lax.erf(v * 0.7071067811865476))
    slope = half + v * jnp.exp(-0.5 * v * v) * 0.3989422804014327
    return v * half, slope


LINES = 4
CHUNKS = 2


def follow(value, done):
    return lax.optimization_barrier((value, done))


def line_groups(cols):
    return [[z * cols + x for z in range(LINES)] for x in range(cols)]


def col_groups(cols):
    return [[z * cols + x for x in range(cols)] for z in range(LINES)]


def line_step(arr, cols, hop, reach):
    if hop > 0:
        lines = range(reach - 1, LINES - 1)
        pairs = [(z * cols + x, (z + 1) * cols + x) for z in lines for x in range(cols)]
    else:
        lines = range(1, LINES - reach + 1)
        pairs = [(z * cols + x, (z - 1) * cols + x) for z in lines for x in range(cols)]
    return lax.ppermute(arr, "tensor", pairs)


def line_gather(own, cols, line):
    ups, downs = [own], [own]
    for reach in range(1, LINES):
        ups.append(line_step(ups[-1], cols, 1, reach))
        downs.append(line_step(downs[-1], cols, -1, reach))
    slots = [own]
    for r in range(1, LINES):
        slots.append(jnp.where(line >= r, ups[r], downs[LINES - r]))
    return slots, ups[1]


def line_pairs(cols, hop, far):
    if hop > 0:
        lines = range(0, LINES - far)
    else:
        lines = range(far, LINES)
    return [(z * cols + x, (z + hop) * cols + x) for z in lines for x in range(cols)]


def line_scatter(parts, cols):
    up = down = None
    for far in range(LINES - 1, 0, -1):
        u, d = parts[LINES - far], parts[far]
        if up is not None:
            u, d = u + up, d + down
        up = lax.ppermute(u, "tensor", line_pairs(cols, 1, far))
        down = lax.ppermute(d, "tensor", line_pairs(cols, -1, far))
        if far == 2:
            mark = up
    return parts[0] + (up + down), mark


def turn(arr, line):
    flipped = arr[::-1]
    twice = jnp.concatenate([flipped, flipped], axis=0)
    return lax.dynamic_slice_in_dim(twice, LINES - 1 - line, LINES, axis=0)


def to_col(units, cols, own):
    tok = units.shape[3]
    parts = units.reshape(LINES, own, cols, own, HB // NB, tok).transpose(2, 0, 1, 3, 4, 5)
    got = lax.all_to_all(
        parts, "tensor", 0, 0, axis_index_groups=col_groups(cols), tiled=True
    )
    return got.transpose(3, 1, 0, 2, 4, 5).reshape(own, HB, tok)


def from_col(units, cols, own):
    tok = units.shape[2]
    parts = units.reshape(own, LINES, cols, own, HB // NB, tok).transpose(2, 1, 3, 0, 4, 5)
    got = lax.all_to_all(
        parts, "tensor", 0, 0, axis_index_groups=col_groups(cols), tiled=True
    )
    return got.transpose(1, 2, 0, 3, 4, 5).reshape(LINES, own, HB // LINES, tok)


def line_swap(arr, cols):
    return lax.all_to_all(arr, "tensor", 0, 0, axis_index_groups=line_groups(cols), tiled=True)


def scatter(grad, axis):
    return lax.psum_scatter(grad, "fsdp", scatter_dimension=axis, tiled=True)


def local(activations, first_factor, second_factor, third_factor, fourth_factor, out_grad):
    tok = activations.shape[0]
    own = second_factor.shape[0]
    block_in = D // NB
    cols = NB // own // LINES
    wide = HB // LINES
    line = lax.axis_index("tensor") // cols
    step = tok // CHUNKS

    rows = first_factor.shape[1]
    wone = first_factor.reshape(own, rows, LINES, wide).transpose(2, 0, 1, 3)
    wone = turn(line_swap(wone, cols), line)
    wone = lax.all_gather(wone, "fsdp", axis=2, tiled=True)

    gathered = []
    last = None
    for n in range(CHUNKS):
        for arr in (activations, out_grad):
            shard = arr[n * step : (n + 1) * step]
            if last is not None:
                shard, gate = follow(shard, last[1])
            slots, mark = line_gather(shard, cols, line)
            last = (slots, mark)
            gathered.append([v.reshape(step, own, block_in) for v in slots])

    wfour = lax.all_gather(fourth_factor, "fsdp", axis=1, tiled=True)
    wfour = wfour.reshape(own, LINES, wide, block_in).transpose(1, 0, 2, 3)
    wfour = turn(line_swap(wfour, cols), line)
    wtwo = lax.all_gather(second_factor, "fsdp", axis=1, tiled=True)
    wthree = lax.all_gather(third_factor, "fsdp", axis=1, tiled=True)
    wtwo = turn(
        wtwo.reshape(own, LINES, wide, HB).transpose(1, 0, 2, 3), line
    ).transpose(1, 0, 2, 3).reshape(own, HB, HB)
    wthree = turn(
        wthree.reshape(own, HB, LINES, wide).transpose(2, 0, 1, 3), line
    ).transpose(1, 2, 0, 3).reshape(own, HB, HB)

    results, in_grads = [], []
    sums = [0.0, 0.0, 0.0, 0.0]
    for n in range(CHUNKS):
        xg = jnp.stack(gathered[2 * n])
        gg = jnp.stack(gathered[2 * n + 1])
        out = jnp.einsum("ztbi,zbij->zbjt", xg, wone, preferred_element_type=F32).astype(BF16)
        if n:
            out, regrouped = follow(out, regrouped)
        mixed = to_col(out, cols, own)
        dw = jnp.einsum("ztbo,zbpo->zbpt", gg, wfour, preferred_element_type=F32).astype(BF16)
        ddown = to_col(dw, cols, own)
        pre = jnp.einsum("cpt,cpm->cmt", mixed, wtwo, preferred_element_type=F32)
        act, slope = gelu_both(pre)
        hidden = act.astype(BF16)
        down = jnp.einsum("cmt,cmn->cnt", hidden, wthree, preferred_element_type=F32)
        down = down.astype(BF16)
        if n:
            down, results[-1][1] = follow(down, results[-1][1])
        regrouped = from_col(down, cols, own)
        dhidden = jnp.einsum("cnt,cmn->cmt", ddown, wthree, preferred_element_type=F32)
        dpre = (dhidden * slope).astype(BF16)
        dz = jnp.einsum("cmt,cpm->cpt", dpre, wtwo, preferred_element_type=F32).astype(BF16)
        if n:
            dz, in_grads[-1][1] = follow(dz, in_grads[-1][1])
        dy = from_col(dz, cols, own)
        res = jnp.einsum("zbpt,zbpo->ztbo", regrouped, wfour, preferred_element_type=F32)
        res = res.astype(BF16).reshape(LINES, step, own * block_in)
        results.append(list(line_scatter([res[r] for r in range(LINES)], cols)))
        ing = jnp.einsum("zbjt,zbij->ztbi", dy, wone, preferred_element_type=F32)
        ing = ing.astype(BF16).reshape(LINES, step, own * block_in)
        in_grads.append(list(line_scatter([ing[r] for r in range(LINES)], cols)))
        terms = (
            jnp.einsum("ztbi,zbjt->zbij", xg, dy, preferred_element_type=F32),
            jnp.einsum("cpt,cmt->cpm", mixed, dpre, preferred_element_type=F32),
            jnp.einsum("cmt,cnt->cmn", hidden, ddown, preferred_element_type=F32),
            jnp.einsum("zbpt,ztbo->zbpo", regrouped, gg, preferred_element_type=F32),
        )
        sums = [a + b for a, b in zip(sums, terms)]
    first_grad = scatter(turn(sums[0].astype(BF16), line), 2)
    first_grad = line_swap(first_grad, cols).transpose(1, 2, 0, 3).reshape(own, rows, HB)
    second_grad = turn(
        sums[1].astype(BF16).reshape(own, LINES, wide, HB).transpose(1, 0, 2, 3), line
    ).transpose(1, 0, 2, 3).reshape(own, HB, HB)
    third_grad = turn(
        sums[2].astype(BF16).reshape(own, HB, LINES, wide).transpose(2, 0, 1, 3), line
    ).transpose(1, 2, 0, 3).reshape(own, HB, HB)
    fourth_grad = line_swap(turn(sums[3].astype(BF16), line), cols)
    fourth_grad = fourth_grad.transpose(1, 0, 2, 3).reshape(own, HB, block_in)
    return (
        jnp.concatenate([r[0] for r in results], axis=0),
        jnp.concatenate([r[0] for r in in_grads], axis=0),
        first_grad.astype(F32),
        scatter(second_grad, 1).astype(F32),
        scatter(third_grad, 1).astype(F32),
        scatter(fourth_grad, 1).astype(F32),
    )


def solution(mesh):
    in_specs = (
        P("fsdp", "tensor"),
        P("tensor", "fsdp", None),
        P("tensor", "fsdp", None),
        P("tensor", "fsdp", None),
        P("tensor", "fsdp", None),
        P("fsdp", "tensor"),
    )
    out_specs = (
        P("fsdp", "tensor"),
        P("fsdp", "tensor"),
        P("tensor", "fsdp", None),
        P("tensor", "fsdp", None),
        P("tensor", "fsdp", None),
        P("tensor", "fsdp", None),
    )
    return jax.shard_map(local, mesh=mesh, in_specs=in_specs, out_specs=out_specs, check_vma=False)
```

time: 852 us -> 996 us (1.17)
  waiting for transfers between devices: 545 us -> 347 us
  starting transfers between devices: 47.4 us -> 190 us
  local copies, waits for them, and re-layouts: 87.8 us -> 194 us
  other arithmetic: 18.2 us -> 96.2 us
  blocking collectives: 14 us -> 33.7 us
    all_to_all x6 -> x11, waiting for transfers between devices: 484 us -> 103 us  [the longest x4 57.6 us: from_col(): lax.all_to_all(parts, 'tensor', 0, 0, axis_index_groups=col_groups(cols),...]
    ppermute x0 -> x48, waiting for transfers between devices: none -> 242 us  [the longest x24 105 us: line_step(): return lax.ppermute(arr, 'tensor', pairs)]
    ppermute x0 -> x48, starting transfers between devices: none -> 130 us  [the longest x24 77.8 us: line_step(): return lax.ppermute(arr, 'tensor', pairs)]
    all_gather x3 -> x4, waiting for transfers between devices: 59.3 us -> 0.03 us  [the longest x1 0.02 us: local(): wtwo = lax.all_gather(second_factor, 'fsdp', axis=1, tiled=True)]
    add x0 -> x16, other arithmetic: none -> 41.6 us  [the longest x12 32.4 us: line_scatter(): u, d = (u + up, d + down)]
    rev x0 -> x8, local copies, waits for them, and re-layouts: none -> 36.8 us  [turn(): flipped = arr[::-1]]
    all_to_all x0 -> x1, blocking collectives: none -> 33.7 us  [line_swap(): lax.all_to_all(arr, 'tensor', 0, 0, axis_index_groups=line_groups(cols),...]
    another operation x0 -> x16, local copies, waits for them, and re-layouts: none -> 25.8 us  [the longest x8 14.3 us: local(): xg = jnp.stack(gathered[2 * n])]
  transfers between devices with their start and end apart: 13 -> 67, of which waited for: 9 -> 28; matrix products, arithmetic and copies ran while one was open for 24% -> 38% of each run, Pallas kernels for 0% -> 0%
where the time goes in v2:
time: 996 us; the launch traced here: 983 us
  waiting for transfers between devices  347 us (35%)
  local copies, waits for them, and re-layouts  194 us (19%)
  starting transfers between devices  190 us (19%)
  matrix products  107 us (11%)
  other arithmetic  96.2 us (10%)
  blocking collectives  33.7 us (3%)
  between operations  15.9 us (2%)
    ppermute x24, waiting for transfers between devices, line_step(): return lax.ppermute(arr, 'tensor', pairs)  105 us
    ppermute x12, waiting for transfers between devices, line_scatter(): down = lax.ppermute(d, 'tensor', line_pairs(cols, -1, far))  102 us
    ppermute x24, starting transfers between devices, line_step(): return lax.ppermute(arr, 'tensor', pairs)  77.8 us
    all_to_all x4, waiting for transfers between devices, from_col(): lax.all_to_all(parts, 'tensor', 0, 0, axis_index_groups=col_groups(cols),...  57.6 us
    rev x8, local copies, waits for them, and re-layouts, turn(): flipped = arr[::-1]  36.8 us
    ppermute x12, waiting for transfers between devices, line_scatter(): up = lax.ppermute(u, 'tensor', line_pairs(cols, 1, far))  35.9 us
    all_to_all x1, blocking collectives, line_swap(): lax.all_to_all(arr, 'tensor', 0, 0, axis_index_groups=line_groups(cols),...  33.7 us
    add x12, other arithmetic, line_scatter(): u, d = (u + up, d + down)  32.4 us
  transfers between devices with their start and end apart: 67, of which 28 were waited for; matrix products, arithmetic and copies ran while one was open for 38% of the time, Pallas kernels for 0%

profile of v2, /device:TPU:16, one launch (start us, length us, event | category | flops | bytes accessed | tf_op | source)
XLA Modules:
  0.0 983.2 jit_solution(17848338177603315445)
XLA Ops:
  30.7 19.0 %collective-permute-done.1 = bf16[512,1024]{0,1:T(8,128)(2,1)} collective-permute-done((bf16[512,1024]{0,1:T(8,128)(2,1)S(1)}, bf16[512,1024]{0,1:T(8,128)(2,1)}, u32[]{:S(2)}, u32[]{:S(2)}) %collective-permute-start.1) | collective-permute-done | bytes 1048608 | tf_op jit(solution)/shard_map/ppermute | solution.py:42
  66.0 10.8 %collective-permute-done.2 = bf16[512,1024]{0,1:T(8,128)(2,1)} collective-permute-done((bf16[512,1024]{0,1:T(8,128)(2,1)}, bf16[512,1024]{0,1:T(8,128)(2,1)}, u32[]{:S(2)}, u32[]{:S(2)}) %collective-permute-start.2) | collective-permute-done | bytes 1048608 | tf_op jit(solution)/shard_map/ppermute | solution.py:42
  86.2 16.4 %collective-permute-done.12 = bf16[512,1024]{0,1:T(8,128)(2,1)} collective-permute-done((bf16[512,1024]{0,1:T(8,128)(2,1)S(1)}, bf16[512,1024]{0,1:T(8,128)(2,1)}, u32[]{:S(2)}, u32[]{:S(2)}) %collective-permute-start.12) | collective-permute-done | bytes 1048608 | tf_op jit(solution)/shard_map/ppermute | solution.py:42
  137.6 21.2 %collective-permute-done.13 = bf16[512,1024]{0,1:T(8,128)(2,1)} collective-permute-done((bf16[512,1024]{0,1:T(8,128)(2,1)S(1)}, bf16[512,1024]{0,1:T(8,128)(2,1)}, u32[]{:S(2)}, u32[]{:S(2)}) %collective-permute-start.13) | collective-permute-done | bytes 1048608 | tf_op jit(solution)/shard_map/ppermute | solution.py:42
  175.3 8.3 collective-permute-done.28
  220.6 9.5 collective-permute-done.36
  254.3 20.0 %rev.26 = bf16[4,8,128,512]{2,0,3,1:T(4,128)(2,1)} reverse(bf16[4,8,128,512]{2,0,3,1:T(4,128)(2,1)} %bitcast.192), dimensions={0} | reverse | bytes 8388608 | tf_op jit(solution)/shard_map/rev | solution.py:78
  274.2 10.9 %fusion.15 = bf16[8,4,128,512]{2,1,3,0:T(4,128)(2,1)} fusion(s32[]{:T(128)S(6)} %select_n.72, bf16[4,8,128,512]{2,0,3,1:T(4,128)(2,1)} %rev.26), kind=kLoop, calls=%fused_computation.31 | loop fusion | flops 8388608 | bytes 8388612 | tf_op jit(solution)/shard_map/transpose | solution.py:141
  328.4 10.0 %collective-permute-start.15 = (bf16[512,1024]{0,1:T(8,128)(2,1)}, bf16[512,1024]{0,1:T(8,128)(2,1)}, u32[]{:S(2)}, u32[]{:S(2)}) collective-permute-start(bf16[512,1024]{0,1:T(8,128)(2,1)} %collective-permute-done.14), channel_id=1, source_target_pairs={{2,0},{3,1},{4,2},{5,3},{10,8},{11,9},{12,10},{13,11},{18,16},{19,... | collective-permute-start | bytes 3145736 | tf_op jit(solution)/shard_map/ppermute | solution.py:42
  352.4 14.8 %all-to-all-done.3 = bf16[2,4,8,8,8,512]{5,4,2,1,3,0:T(8,128)(2,1)} async-done(((bf16[2,4,8,8,8,512]{5,4,2,1,3,0:T(8,128)(2,1)}), bf16[2,4,8,8,8,512]{5,4,2,1,3,0:T(8,128)(2,1)}, u32[]{:S(2)}, u32[]{:S(2)}) %all-to-all-start.3) | async-done | bytes 4194336 | tf_op jit(solution)/shard_map/all_to_all | solution.py:95
  380.1 9.6 fusion.5
  396.6 18.7 %all-to-all-done.8 = bf16[2,4,8,8,8,512]{5,4,3,2,1,0:T(8,128)(2,1)} async-done(((bf16[2,4,8,8,8,512]{5,4,3,2,1,0:T(8,128)(2,1)}), bf16[2,4,8,8,8,512]{5,4,3,2,1,0:T(8,128)(2,1)}, u32[]{:S(2)}, u32[]{:S(2)}) %all-to-all-start.8) | async-done | bytes 4194336 | tf_op jit(solution)/shard_map/all_to_all | solution.py:86
  430.4 9.2 collective-permute-done.18
  453.1 9.3 all-to-all-done.7
  519.7 11.7 %collective-permute-done.7 = bf16[512,1024]{1,0:T(8,128)(2,1)S(1)} collective-permute-done((bf16[512,1024]{1,0:T(8,128)(2,1)S(1)}, bf16[512,1024]{1,0:T(8,128)(2,1)S(1)}, u32[]{:S(2)}, u32[]{:S(2)}) %collective-permute-start.7) | collective-permute-done | bytes 1048608 | tf_op jit(solution)/shard_map/ppermute | solution.py:70
  554.3 24.2 %collective-permute-done.31 = bf16[512,1024]{1,0:T(8,128)(2,1)S(1)} collective-permute-done((bf16[512,1024]{1,0:T(8,128)(2,1)S(1)}, bf16[512,1024]{1,0:T(8,128)(2,1)S(1)}, u32[]{:S(2)}, u32[]{:S(2)}) %collective-permute-start.31) | collective-permute-done | bytes 1048608 | tf_op jit(solution)/shard_map/ppermute | solution.py:70
  595.0 33.5 %all-to-all-done.9 = bf16[2,4,8,8,8,512]{5,4,2,1,3,0:T(8,128)(2,1)} async-done(((bf16[2,4,8,8,8,512]{5,4,2,1,3,0:T(8,128)(2,1)}), bf16[2,4,8,8,8,512]{5,4,2,1,3,0:T(8,128)(2,1)}, u32[]{:S(2)}, u32[]{:S(2)}) %all-to-all-start.9) | async-done | bytes 4194336 | tf_op jit(solution)/shard_map/all_to_all | solution.py:95
  649.1 33.7 %all_to_all.60 = bf16[4,8,128,128]{3,2,1,0:T(8,128)(2,1)S(1)} all-to-all(bf16[4,8,128,128]{3,2,1,0:T(8,128)(2,1)S(1)} %fusion.17), channel_id=1, replica_groups={{0,2,4,6},{1,3,5,7},{8,10,12,14},{9,11,13,15},{16,18,20,22},{17,19,21,2..., dimensions={0} | all-to-all | bytes 2097152 | tf_op jit(solution)/shard_map/all_to_all | solution.py:102
  796.0 12.0 %collective-permute-done.22 = bf16[512,1024]{1,0:T(8,128)(2,1)} collective-permute-done((bf16[512,1024]{1,0:T(8,128)(2,1)S(1)}, bf16[512,1024]{1,0:T(8,128)(2,1)}, u32[]{:S(2)}, u32[]{:S(2)}) %collective-permute-start.22) | collective-permute-done | bytes 1048608 | tf_op jit(solution)/shard_map/ppermute | solution.py:71
  812.9 17.5 %collective-permute-done.10 = bf16[512,1024]{1,0:T(8,128)(2,1)} collective-permute-done((bf16[512,1024]{1,0:T(8,128)(2,1)}, bf16[512,1024]{1,0:T(8,128)(2,1)}, u32[]{:S(2)}, u32[]{:S(2)}) %collective-permute-start.10) | collective-permute-done | bytes 1048608 | tf_op jit(solution)/shard_map/ppermute | solution.py:71
  833.8 19.2 %collective-permute-done.35 = bf16[512,1024]{1,0:T(8,128)(2,1)} collective-permute-done((bf16[512,1024]{1,0:T(8,128)(2,1)}, bf16[512,1024]{1,0:T(8,128)(2,1)}, u32[]{:S(2)}, u32[]{:S(2)}) %collective-permute-start.35) | collective-permute-done | bytes 1048608 | tf_op jit(solution)/shard_map/ppermute | solution.py:71
  857.1 18.4 %collective-permute-done.46 = bf16[512,1024]{1,0:T(8,128)(2,1)} collective-permute-done((bf16[512,1024]{1,0:T(8,128)(2,1)}, bf16[512,1024]{1,0:T(8,128)(2,1)}, u32[]{:S(2)}, u32[]{:S(2)}) %collective-permute-start.46) | collective-permute-done | bytes 1048608 | tf_op jit(solution)/shard_map/ppermute | solution.py:71
  928.3 17.3 %all-to-all-done.10 = bf16[4,8,32,128]{3,2,1,0:T(8,128)(2,1)S(1)} async-done(((bf16[4,8,32,128]{3,2,1,0:T(8,128)(2,1)}), bf16[4,8,32,128]{3,2,1,0:T(8,128)(2,1)S(1)}, u32[]{:S(2)}, u32[]{:S(2)}) %all-to-all-start.10) | async-done | bytes 262176 | tf_op jit(solution)/shard_map/all_to_all | solution.py:102
  949.7 15.4 %collective-permute-done.24 = bf16[512,1024]{1,0:T(8,128)(2,1)} collective-permute-done((bf16[512,1024]{1,0:T(8,128)(2,1)}, bf16[512,1024]{1,0:T(8,128)(2,1)}, u32[]{:S(2)}, u32[]{:S(2)}) %collective-permute-start.24) | collective-permute-done | bytes 1048608 | tf_op jit(solution)/shard_map/ppermute | solution.py:71
  (374 shorter events, 576.7 us)
Async XLA Ops:
  7.2 102.3 %all-gather.5.cloned.1.call-start = ((), (), s32[]{:S(2)}) async-start(), calls=%async_computation.16 | async-start | bytes 1310720 | tf_op jit(solution)/shard_map/all_gather | solution.py:134
  14.1 148.3 %all-gather.11.cloned.1.call-start = ((), (), s32[]{:S(2)}) async-start(), calls=%async_computation.19 | async-start | bytes 1310720 | tf_op jit(solution)/shard_map/all_gather | solution.py:121
  20.8 226.0 %all-gather.9.cloned.1.call-start = ((), (), s32[]{:S(2)}) async-start(), calls=%async_computation.18 | async-start | bytes 5242880 | tf_op jit(solution)/shard_map/all_gather | solution.py:137
  21.5 270.9 %all-gather.7.cloned.1.call-start = ((), (), s32[]{:S(2)}) async-start(), calls=%async_computation.17 | async-start | bytes 5242880 | tf_op jit(solution)/shard_map/all_gather | solution.py:138
  102.6 56.2 %collective-permute-start.13 = (bf16[512,1024]{0,1:T(8,128)(2,1)S(1)}, bf16[512,1024]{0,1:T(8,128)(2,1)}, u32[]{:S(2)}, u32[]{:S(2)}) collective-permute-start(bf16[512,1024]{0,1:T(8,128)(2,1)S(1)} %copy.220), channel_id=1, source_target_pairs={{0,2},{1,3},{2,4},{3,5},{4,6},{5,7},{8,10},{9,11},{10,12},{11,13},... | collective-permute-start | bytes 3145736 | tf_op jit(solution)/shard_map/ppermute | solution.py:42
  111.7 57.0 %all-to-all-start = ((bf16[4,8,128,128]{2,3,1,0:T(8,128)(2,1)}), bf16[4,8,128,128]{2,3,1,0:T(8,128)(2,1)S(1)}, u32[]{:S(2)}, u32[]{:S(2)}) async-start(bf16[4,8,128,128]{2,3,1,0:T(8,128)(2,1)} %bitcast.216), calls=%async_computation | async-start | bytes 2097152 | tf_op jit(solution)/shard_map/all_to_all | solution.py:102
  125.0 58.6 %collective-permute-start.28 = (bf16[512,1024]{0,1:T(8,128)(2,1)}, bf16[512,1024]{0,1:T(8,128)(2,1)}, u32[]{:S(2)}, u32[]{:S(2)}) collective-permute-start(bf16[512,1024]{0,1:T(8,128)(2,1)} %collective-permute-done.12), channel_id=1, source_target_pairs={{2,4},{3,5},{4,6},{5,7},{10,12},{11,13},{12,14},{13,15},{18,20},{1... | collective-permute-start | bytes 3145736 | tf_op jit(solution)/shard_map/ppermute | solution.py:42
  169.7 64.8 %all-to-all-start.2 = ((bf16[2,4,8,8,8,512]{5,4,3,2,1,0:T(8,128)(2,1)}), bf16[2,4,8,8,8,512]{5,4,3,2,1,0:T(8,128)(2,1)}, u32[]{:S(2)}, u32[]{:S(2)}) async-start(bf16[2,4,8,8,8,512]{5,4,3,2,1,0:T(8,128)(2,1)} %bitcast.185), calls=%async_computation.2 | async-start | bytes 8388608 | tf_op jit(solution)/shard_map/all_to_all | solution.py:86
  190.3 138.1 %collective-permute-start.14 = (bf16[512,1024]{0,1:T(8,128)(2,1)S(1)}, bf16[512,1024]{0,1:T(8,128)(2,1)}, u32[]{:S(2)}, u32[]{:S(2)}) collective-permute-start(bf16[512,1024]{0,1:T(8,128)(2,1)S(1)} %copy.220), channel_id=1, source_target_pairs={{2,0},{3,1},{4,2},{5,3},{6,4},{7,5},{10,8},{11,9},{12,10},{13,11},... | collective-permute-start | bytes 3145736 | tf_op jit(solution)/shard_map/ppermute | solution.py:42
  230.1 93.8 %collective-permute-start.40 = (bf16[512,1024]{0,1:T(8,128)(2,1)}, bf16[512,1024]{0,1:T(8,128)(2,1)}, u32[]{:S(2)}, u32[]{:S(2)}) collective-permute-start(bf16[512,1024]{0,1:T(8,128)(2,1)} %collective-permute-done.36), channel_id=1, source_target_pairs={{2,4},{3,5},{4,6},{5,7},{10,12},{11,13},{12,14},{13,15},{18,20},{1... | collective-permute-start | bytes 3145736 | tf_op jit(solution)/shard_map/ppermute | solution.py:42
  234.5 83.8 %all-to-all-start.6 = ((bf16[2,4,8,8,8,512]{5,4,3,2,1,0:T(8,128)(2,1)}), bf16[2,4,8,8,8,512]{5,4,3,2,1,0:T(8,128)(2,1)}, u32[]{:S(2)}, u32[]{:S(2)}) async-start(bf16[2,4,8,8,8,512]{5,4,3,2,1,0:T(8,128)(2,1)} %bitcast.186), calls=%async_computation.6 | async-start | bytes 8388608 | tf_op jit(solution)/shard_map/all_to_all | solution.py:86
  245.0 96.1 %collective-permute-start.39 = (bf16[512,1024]{0,1:T(8,128)(2,1)}, bf16[512,1024]{0,1:T(8,128)(2,1)}, u32[]{:S(2)}, u32[]{:S(2)}) collective-permute-start(bf16[512,1024]{0,1:T(8,128)(2,1)} %collective-permute-done.38), channel_id=1, source_target_pairs={{2,0},{3,1},{10,8},{11,9},{18,16},{19,17},{26,24},{27,25}} | collective-permute-start | bytes 3145736 | tf_op jit(solution)/shard_map/ppermute | solution.py:42
  587.4 315.3 %reduce-scatter.5.cloned.1.call-start = ((), (), s32[]{:S(2)}) async-start(), calls=%async_computation.20 | async-start | bytes 1310720 | tf_op jit(solution)/shard_map/reduce_scatter | solution.py:106
  641.6 326.9 %reduce-scatter.11.cloned.1.call-start = ((), (), s32[]{:S(2)}) async-start(), calls=%async_computation.23 | async-start | bytes 1310720 | tf_op jit(solution)/shard_map/reduce_scatter | solution.py:106
  683.9 286.4 %reduce-scatter.9.cloned.1.call-start = ((), (), s32[]{:S(2)}) async-start(), calls=%async_computation.22 | async-start | bytes 5242880 | tf_op jit(solution)/shard_map/reduce_scatter | solution.py:106
  712.4 260.7 %reduce-scatter.7.cloned.1.call-start = ((), (), s32[]{:S(2)}) async-start(), calls=%async_computation.21 | async-start | bytes 5242880 | tf_op jit(solution)/shard_map/reduce_scatter | solution.py:106
  763.1 67.4 %collective-permute-start.10 = (bf16[512,1024]{1,0:T(8,128)(2,1)}, bf16[512,1024]{1,0:T(8,128)(2,1)}, u32[]{:S(2)}, u32[]{:S(2)}) collective-permute-start(bf16[512,1024]{1,0:T(8,128)(2,1)} %get-tuple-element.42), channel_id=1, source_target_pairs={{4,2},{5,3},{6,4},{7,5},{12,10},{13,11},{14,12},{15,13},{20,18},{2... | collective-permute-start | bytes 3145736 | tf_op jit(solution)/shard_map/ppermute | solution.py:71
  771.1 81.8 %collective-permute-start.35 = (bf16[512,1024]{1,0:T(8,128)(2,1)}, bf16[512,1024]{1,0:T(8,128)(2,1)}, u32[]{:S(2)}, u32[]{:S(2)}) collective-permute-start(bf16[512,1024]{1,0:T(8,128)(2,1)} %add.135), channel_id=1, source_target_pairs={{2,0},{3,1},{4,2},{5,3},{6,4},{7,5},{10,8},{11,9},{12,10},{13,11},... | collective-permute-start | bytes 3145736 | tf_op jit(solution)/shard_map/ppermute | solution.py:71
  789.0 86.5 %collective-permute-start.46 = (bf16[512,1024]{1,0:T(8,128)(2,1)}, bf16[512,1024]{1,0:T(8,128)(2,1)}, u32[]{:S(2)}, u32[]{:S(2)}) collective-permute-start(bf16[512,1024]{1,0:T(8,128)(2,1)} %get-tuple-element.40), channel_id=1, source_target_pairs={{4,2},{5,3},{6,4},{7,5},{12,10},{13,11},{14,12},{15,13},{20,18},{2... | collective-permute-start | bytes 3145736 | tf_op jit(solution)/shard_map/ppermute | solution.py:71
  790.9 86.5 %collective-permute-start.43 = (bf16[512,1024]{1,0:T(8,128)(2,1)}, bf16[512,1024]{1,0:T(8,128)(2,1)}, u32[]{:S(2)}, u32[]{:S(2)}) collective-permute-start(bf16[512,1024]{1,0:T(8,128)(2,1)} %get-tuple-element.41), channel_id=1, source_target_pairs={{0,2},{1,3},{2,4},{3,5},{8,10},{9,11},{10,12},{11,13},{16,18},{17,... | collective-permute-start | bytes 3145736 | tf_op jit(solution)/shard_map/ppermute | solution.py:70
  808.0 80.1 %collective-permute-start.32 = (bf16[512,1024]{1,0:T(8,128)(2,1)}, bf16[512,1024]{1,0:T(8,128)(2,1)S(1)}, u32[]{:S(2)}, u32[]{:S(2)}) collective-permute-start(bf16[512,1024]{1,0:T(8,128)(2,1)} %add.133), channel_id=1, source_target_pairs={{0,2},{1,3},{2,4},{3,5},{4,6},{5,7},{8,10},{9,11},{10,12},{11,13},... | collective-permute-start | bytes 3145736 | tf_op jit(solution)/shard_map/ppermute | solution.py:70
  830.5 67.4 %collective-permute-start.23 = (bf16[512,1024]{1,0:T(8,128)(2,1)S(1)}, bf16[512,1024]{1,0:T(8,128)(2,1)}, u32[]{:S(2)}, u32[]{:S(2)}) collective-permute-start(bf16[512,1024]{1,0:T(8,128)(2,1)S(1)} %get-tuple-element.44), channel_id=1, source_target_pairs={{4,2},{5,3},{6,4},{7,5},{12,10},{13,11},{14,12},{15,13},{20,18},{2... | collective-permute-start | bytes 3145736 | tf_op jit(solution)/shard_map/ppermute | solution.py:71
  853.0 60.1 %collective-permute-start.20 = (bf16[512,1024]{1,0:T(8,128)(2,1)}, bf16[512,1024]{1,0:T(8,128)(2,1)}, u32[]{:S(2)}, u32[]{:S(2)}) collective-permute-start(bf16[512,1024]{1,0:T(8,128)(2,1)} %get-tuple-element.45), channel_id=1, source_target_pairs={{0,2},{1,3},{2,4},{3,5},{8,10},{9,11},{10,12},{11,13},{16,18},{17,... | collective-permute-start | bytes 3145736 | tf_op jit(solution)/shard_map/ppermute | solution.py:70
  888.1 58.3 %collective-permute-start.47 = (bf16[512,1024]{1,0:T(8,128)(2,1)}, bf16[512,1024]{1,0:T(8,128)(2,1)}, u32[]{:S(2)}, u32[]{:S(2)}) collective-permute-start(bf16[512,1024]{1,0:T(8,128)(2,1)} %add.142), channel_id=1, source_target_pairs={{2,0},{3,1},{4,2},{5,3},{6,4},{7,5},{10,8},{11,9},{12,10},{13,11},... | collective-permute-start | bytes 3145736 | tf_op jit(solution)/shard_map/ppermute | solution.py:71
  (101 other events, 2502.0 us)
Sparse Core Ops, SparseCore 0:
  9.6 17.7 all-gather.4
  29.5 16.7 all-gather.10
  47.9 34.4 all-gather.8
  83.8 34.4 all-gather.6
  641.7 38.4 reduce-scatter.4
  684.0 25.1 reduce-scatter.10
  712.5 44.8 reduce-scatter.8
  760.1 44.5 reduce-scatter.6
